TPU v7x, 256 devices: a whole 4x4x8 slice. The times are simulated.
256 devices in a mesh: prow: 8 (over z_lo, y), pcol: 32 (over z_hi, x, core).
Axes of the slice: x: 4, y: 4, z: 8 (z_hi: 4, z_lo: 2; z = z_hi * 2 + z_lo), core: 2. Of those that a mesh axis runs over, the one named last changes fastest.
Arguments:
- ancestor_inverse: bfloat16 [24576, 24576], P('prow', 'pcol'), may hold values from -6 to 6
- tile_pattern: int32 [64, 64], replicated, may hold values 0 or 1
- rows_first: int32 [24576], replicated, may hold values 0 or 1
- rows_second: int32 [24576], replicated, may hold values 0 or 1
- panel_first: bfloat16 [24576, 512], P('prow', 'pcol'), may hold values from -0.0390625 to 0.0390625
- panel_second: bfloat16 [24576, 512], P('prow', 'pcol'), may hold values from -0.21875 to 0.21875
- inner_panel: bfloat16 [512, 512], replicated, may hold values from -0.25 to 0.25
- pivot_first: float32 [512, 512], replicated, may hold values from -6 to 6
- pivot_second: float32 [512, 512], replicated, may hold values from -6 to 6
Outputs:
- column_first: bfloat16 [24576, 512], P(('prow', 'pcol'))
- diagonal_first: float32 [512, 512], replicated
- inner_second: float32 [512, 512], replicated
- column_second: bfloat16 [24576, 512], P(('prow', 'pcol'))
- diagonal_second: float32 [512, 512], replicated
Inputs may be any that keep to these rules, and one draw needn't show every extreme that they name: `tile_pattern`: 1 marks a structurally nonzero tile. `rows_first`: 1 marks a row of the first supernode's structure. By construction here, a row belongs to the second supernode's structure only where both rows_second and rows_first are 1.
All inputs are finite; a program needn't handle non-finite values.
Results may differ from a plain program's by a relative error of at most 0.015.
Values may be sent and summed in bfloat16 or wider, within the bound.
A program may use at most 128 MiB of HBM per device.

v0:
```python
import jax
import jax.numpy as jnp
from jax import lax
from jax.sharding import PartitionSpec as P

TILE = 384


def from_root(shard, axis, root):
    mine = lax.axis_index(axis) == root
    return lax.psum(jnp.where(mine, shard, jnp.zeros_like(shard)), axis)


def mask_tiles(block, pattern, row_start, col_start):
    tile_rows = block.shape[0] // TILE
    tile_cols = block.shape[1] // TILE
    window = lax.dynamic_slice(pattern, (row_start, col_start), (tile_rows, tile_cols)).astype(
        jnp.bfloat16
    )
    shaped = block.reshape(tile_rows, TILE, tile_cols, TILE) * window[:, None, :, None]
    return shaped.reshape(block.shape)


def body(
    ancestor_inverse,
    tile_pattern,
    rows_first,
    rows_second,
    panel_first,
    panel_second,
    inner_panel,
    pivot_first,
    pivot_second,
):
    row_count = lax.axis_size("prow")
    col_count = lax.axis_size("pcol")
    row_id = lax.axis_index("prow")
    col_id = lax.axis_index("pcol")
    row_block = ancestor_inverse.shape[0]
    col_block = ancestor_inverse.shape[1]
    share = row_block // col_count
    sparse = mask_tiles(
        ancestor_inverse, tile_pattern, row_id * (row_block // TILE), col_id * (col_block // TILE)
    )
    struct_first = lax.dynamic_slice_in_dim(rows_first, row_id * row_block, row_block).astype(
        jnp.bfloat16
    )
    struct_second = struct_first * lax.dynamic_slice_in_dim(
        rows_second, row_id * row_block, row_block
    ).astype(jnp.bfloat16)
    local_first = panel_first * struct_first[:, None]
    local_second = panel_second * struct_second[:, None]
    source = col_id * row_count // col_count
    offset = col_id * col_block - source * row_block

    def summed_terms(columns):
        return jnp.dot(sparse, columns, preferred_element_type=jnp.float32)

    def ancestor_terms(local):
        full = lax.all_gather(local, "pcol", axis=1, tiled=True)
        mirrored = from_root(lax.dynamic_slice_in_dim(full, offset, col_block, 0), "prow", source)
        return (
            full,
            lax.psum_scatter(
                summed_terms(mirrored).astype(jnp.bfloat16), "pcol", scatter_dimension=0, tiled=True
            ).astype(jnp.float32),
        )

    full_first, sum_first = ancestor_terms(local_first)
    full_second, sum_second = ancestor_terms(local_second)
    column_first = (-sum_first).astype(jnp.bfloat16)
    own_first = lax.dynamic_slice_in_dim(full_first, col_id * share, share, 0)
    own_second = lax.dynamic_slice_in_dim(full_second, col_id * share, share, 0)
    corr_first, crossed = lax.psum(
        (
            jnp.dot(own_first.T, column_first, preferred_element_type=jnp.float32),
            jnp.dot(column_first.T, own_second, preferred_element_type=jnp.float32),
        ),
        ("prow", "pcol"),
    )
    diagonal_first = pivot_first - corr_first
    column_second = (
        -(sum_second + jnp.dot(column_first, inner_panel, preferred_element_type=jnp.float32))
    ).astype(jnp.bfloat16)
    inner_wide = inner_panel.astype(jnp.float32)
    inner_second = -(jnp.dot(diagonal_first, inner_wide, precision=lax.Precision.HIGHEST) + crossed)
    corr_second = lax.psum(
        jnp.dot(own_second.T, column_second, preferred_element_type=jnp.float32), ("prow", "pcol")
    )
    diagonal_second = (
        pivot_second
        - jnp.dot(inner_wide.T, inner_second, precision=lax.Precision.HIGHEST)
        - corr_second
    )
    return (column_first, diagonal_first, inner_second, column_second, diagonal_second)


def solution(mesh):
    return jax.shard_map(
        body,
        mesh=mesh,
        in_specs=(
            P("prow", "pcol"),
            P(),
            P(),
            P(),
            P("prow", "pcol"),
            P("prow", "pcol"),
            P(),
            P(),
            P(),
        ),
        out_specs=(P(("prow", "pcol"), None), P(), P(), P(("prow", "pcol"), None), P()),
        check_vma=False,
    )
```

profile of v0, /device:TPU:8, one launch (start us, length us, event | category | flops | bytes accessed | tf_op | source)
XLA Modules:
  0.0 701.2 jit_solution(2915164507721282915)
XLA Ops:
  7.2 0.0 copy-start
  7.2 0.0 all-gather.5.cloned.1.call-start
  7.2 0.8 fusion.13
  8.0 1.5 broadcast_multiply_fusion
  9.6 0.0 all-gather.5.cloned.1.call-update
  9.6 0.0 all-gather.3.cloned.1.call-start
  9.6 1.5 broadcast_multiply_fusion.1
  11.2 0.0 all-gather.3.cloned.1.call-update
  11.2 0.0 all-reduce.7.cloned.1.call-start
  11.3 59.7 %all-gather.5.cloned.1.call-done = bf16[3072,512]{0,1:T(8,128)(2,1)} async-done(((bf16[3072,16]{0,1:T(8,128)(2,1)}), bf16[3072,512]{0,1:T(8,128)(2,1)}) %all-gather.5.cloned.1.call-update) | async-done | bytes 3145744 | tf_op jit(solution)/shard_map/all_gather | solution.py:60
  71.0 2.1 dynamic-slice_select_fusion
  73.2 55.8 %all-gather.3.cloned.1.call-done = bf16[3072,512]{0,1:T(8,128)(2,1)} async-done(((bf16[3072,16]{0,1:T(8,128)(2,1)}), bf16[3072,512]{0,1:T(8,128)(2,1)}) %all-gather.3.cloned.1.call-update) | async-done | bytes 3145744 | tf_op jit(solution)/shard_map/all_gather | solution.py:60
  129.0 2.1 dynamic-slice_select_fusion.1
  131.1 0.0 all-reduce.7.cloned.1.call-update
  131.2 0.0 reduce-scatter.3.cloned.1.call-start
  131.2 0.8 dynamic-slice_convert_fusion.2
  132.0 2.5 mul.55
  134.5 3.0 copy.18
  137.5 76.0 %all-reduce.7.cloned.1.call-done = (bf16[768,512]{0,1:T(8,128)(2,1)}, bf16[768,512]{0,1:T(8,128)(2,1)}) async-done(((bf16[768,512]{0,1:T(8,128)(2,1)}, bf16[768,512]{0,1:T(8,128)(2,1)}), (bf16[768,512]{0,1:T(8,128)(2,1)}, bf16[768,512]{0,1:T(8,128)(2,1)})) %all-reduce.7.cloned.1.call-update) | async-done | bytes 1572880 | tf_op jit(solution)/shard_map/psum | solution.py:11
  213.4 8.4 %convolution_convert_fusion.1 = bf16[3072,512]{1,0:T(8,128)(2,1)} fusion(bf16[768,512]{0,1:T(8,128)(2,1)} %get-tuple-element.13, bf16[3072,768]{1,0:T(8,128)(2,1)} %param.9, bf16[3072,768]{1,0:T(8,128)(2,1)} %bitcast.21), kind=kOutput, calls=%fused_computation.1 | convolution fusion | flops 2419851264 | bytes 13369344 | tf_op jit(solution)/shard_map/dot_general | solution.py:57
  221.8 0.0 reduce-scatter.3.cloned.1.call-update
  221.8 0.0 reduce-scatter.5.cloned.1.call-start
  221.9 7.9 %convolution_convert_fusion = bf16[3072,512]{1,0:T(8,128)(2,1)} fusion(bf16[768,512]{0,1:T(8,128)(2,1)S(1)} %copy-done.9, bf16[3072,768]{1,0:T(8,128)(2,1)} %param.9, bf16[3072,768]{1,0:T(8,128)(2,1)} %bitcast.22), kind=kOutput, calls=%fused_computation | convolution fusion | flops 2419851264 | bytes 13369344 | tf_op jit(solution)/shard_map/dot_general | solution.py:57
  229.8 0.0 reduce-scatter.5.cloned.1.call-update
  229.8 0.0 copy-start.6
  229.8 0.2 all-reduce.5.cloned.1.call-start
  230.0 88.8 %reduce-scatter.3.cloned.1.call-done = bf16[96,512]{1,0:T(8,128)(2,1)} async-done(((bf16[3072,512]{1,0:T(8,128)(2,1)}), bf16[96,512]{1,0:T(8,128)(2,1)}) %reduce-scatter.3.cloned.1.call-update) | async-done | bytes 98320 | tf_op jit(solution)/shard_map/reduce_scatter | solution.py:64
  318.8 0.9 negate_convert_fusion
  319.8 0.0 copy-start.4
  319.8 0.0 copy-start.5
  319.8 2.4 fusion.11
  322.2 2.3 fusion.7
  324.4 91.8 %reduce-scatter.5.cloned.1.call-done = bf16[96,512]{1,0:T(8,128)(2,1)} async-done(((bf16[3072,512]{1,0:T(8,128)(2,1)}), bf16[96,512]{1,0:T(8,128)(2,1)}) %reduce-scatter.5.cloned.1.call-update) | async-done | bytes 98320 | tf_op jit(solution)/shard_map/reduce_scatter | solution.py:64
  416.3 0.0 copy-done
  416.3 1.1 fusion.6
  417.4 0.0 copy-start.8
  417.4 2.4 fusion.9
  419.8 0.0 all-reduce.5.cloned.1.call-update
  419.8 0.0 copy-done.6
  419.8 1.3 copy.14
  421.1 264.4 %all-reduce.5.cloned.1.call-done = (f32[512,512]{1,0:T(8,128)}, f32[512,512]{1,0:T(8,128)}, f32[512,512]{0,1:T(8,128)}) async-done(((f32[512,512]{1,0:T(8,128)}, f32[512,512]{1,0:T(8,128)}, f32[512,512]{0,1:T(8,128)}), (f32[512,512]{1,0:T(8,128)}, f32[512,512]{1,0:T(8,128)}, f32[512,512]{0,1:T(8,128)})) %all-reduce.5.cloned.1.call-update) | async-done | bytes 3145744 | tf_op jit(solution)/shard_map/psum | solution.py:74
  685.6 1.6 sub.18
  687.2 0.0 copy-done.8
  687.2 0.0 copy-start.1
  687.2 2.6 fusion.2
  689.8 0.0 copy-start.2
  689.8 2.0 fusion.4
  691.8 2.5 copy.16
  (10 shorter events, 0.0 us)
Async XLA Ops:
  7.2 409.1 %copy-start = (bf16[512,512]{1,0:T(8,128)(2,1)S(1)}, bf16[512,512]{1,0:T(8,128)(2,1)}, u32[]{:S(2)}) copy-start(bf16[512,512]{1,0:T(8,128)(2,1)} %param.15) | copy-start | bytes 1572868
  7.2 63.8 %all-gather.5.cloned.1.call-start = ((), (), s32[]{:S(2)}) async-start(), calls=%async_computation.4 | async-start | bytes 3244032 | tf_op jit(solution)/shard_map/all_gather | solution.py:60
  9.6 119.4 %all-gather.3.cloned.1.call-start = ((), (), s32[]{:S(2)}) async-start(), calls=%async_computation.2 | async-start | bytes 3244032 | tf_op jit(solution)/shard_map/all_gather | solution.py:60
  11.2 202.2 %all-reduce.7.cloned.1.call-start = ((), (), s32[]{:S(2)}) async-start(), calls=%async_computation.7 | async-start | bytes 3145728 | tf_op jit(solution)/shard_map/psum | solution.py:11
  131.2 187.7 %reduce-scatter.3.cloned.1.call-start = ((), (), s32[]{:S(2)}) async-start(), calls=%async_computation.3 | async-start | bytes 3244032 | tf_op jit(solution)/shard_map/reduce_scatter | solution.py:64
  213.4 8.4 %copy-start.9 = (bf16[768,512]{0,1:T(8,128)(2,1)S(1)}, bf16[768,512]{0,1:T(8,128)(2,1)}, u32[]{:S(2)}) copy-start(bf16[768,512]{0,1:T(8,128)(2,1)} %get-tuple-element.14) | copy-start | bytes 2359300
  221.8 194.4 %reduce-scatter.5.cloned.1.call-start = ((), (), s32[]{:S(2)}) async-start(), calls=%async_computation.5 | async-start | bytes 3244032 | tf_op jit(solution)/shard_map/reduce_scatter | solution.py:64
  229.8 190.0 %copy-start.6 = (f32[512,512]{1,0:T(8,128)S(1)}, f32[512,512]{1,0:T(8,128)}, u32[]{:S(2)}) copy-start(f32[512,512]{1,0:T(8,128)} %param.17) | copy-start | bytes 3145732
  229.8 455.8 %all-reduce.5.cloned.1.call-start = ((), (), s32[]{:S(2)}) async-start(), calls=%async_computation.6 | async-start | bytes 6291456 | tf_op jit(solution)/shard_map/psum | solution.py:74
  319.8 101.4 %copy-start.4 = (bf16[96,512]{1,0:T(8,128)(2,1)}, bf16[96,512]{1,0:T(8,128)(2,1)S(1)}, u32[]{:S(2)}) copy-start(bf16[96,512]{1,0:T(8,128)(2,1)S(1)} %negate_convert_fusion) | copy-start | bytes 294916
  319.8 365.8 %copy-start.5 = (f32[512,512]{1,0:T(8,128)S(1)}, f32[512,512]{1,0:T(8,128)}, u32[]{:S(2)}) copy-start(f32[512,512]{1,0:T(8,128)} %param.16) | copy-start | bytes 3145732
  417.4 269.8 %copy-start.8 = (bf16[96,512]{1,0:T(8,128)(2,1)}, bf16[96,512]{1,0:T(8,128)(2,1)S(1)}, u32[]{:S(2)}) copy-start(bf16[96,512]{1,0:T(8,128)(2,1)S(1)} %fusion.6) | copy-start | bytes 294916
  685.6 4.2 copy-start.3
  685.6 4.2 copy-start.7
  687.2 7.2 %copy-start.1 = (f32[512,512]{1,0:T(8,128)}, f32[512,512]{1,0:T(8,128)S(1)}, u32[]{:S(2)}) copy-start(f32[512,512]{1,0:T(8,128)S(1)} %sub.18) | copy-start | bytes 3145732
  689.8 4.6 copy-start.2
Sparse Core Ops, SparseCore 0:
  11.1 59.8 all-gather.4
  74.1 54.8 all-gather.2
  132.3 81.1 all-reduce.6
  222.0 96.8 reduce-scatter.2
  323.1 93.1 reduce-scatter.4
  422.5 263.0 all-reduce.4
where the time goes:
time: 702 us; the launch traced here: 701 us
  waiting for transfers between devices  637 us (91%)
  matrix products  29 us (4%)
  between operations  14.3 us (2%)
  other arithmetic  11.4 us (2%)
  local copies, waits for them, and re-layouts  9.39 us (1%)
    psum x1, waiting for transfers between devices, body(): lax.psum((jnp.dot(own_first.T, column_first, preferred_element_type=jnp.f...  264 us
    reduce_scatter x2, waiting for transfers between devices, ancestor_terms(): lax.psum_scatter(summed_terms(mirrored).astype(jnp.bfloat16), 'pcol', sca...  181 us
    all_gather x2, waiting for transfers between devices, ancestor_terms(): full = lax.all_gather(local, 'pcol', axis=1, tiled=True)  116 us
    psum x1, waiting for transfers between devices, from_root(): return lax.psum(jnp.where(mine, shard, jnp.zeros_like(shard)), axis)  76 us
    dot_general x2, matrix products, summed_terms(): return jnp.dot(sparse, columns, preferred_element_type=jnp.float32)  16.2 us
  transfers between devices with their start and end apart: 6, of which 6 were waited for; matrix products, arithmetic and copies ran while one was open for 4% of the time, Pallas kernels for 0%

commit v1 on v0

--- a/solution.py
+++ b/solution.py
@@ -72,11 +72,14 @@
     own_first = lax.dynamic_slice_in_dim(full_first, col_id * share, share, 0)
     own_second = lax.dynamic_slice_in_dim(full_second, col_id * share, share, 0)
     corr_first, crossed = lax.psum(
-        (
-            jnp.dot(own_first.T, column_first, preferred_element_type=jnp.float32),
-            jnp.dot(column_first.T, own_second, preferred_element_type=jnp.float32),
+        lax.psum(
+            (
+                jnp.dot(own_first.T, column_first, preferred_element_type=jnp.float32),
+                jnp.dot(column_first.T, own_second, preferred_element_type=jnp.float32),
+            ),
+            "pcol",
         ),
-        ("prow", "pcol"),
+        "prow",
     )
     diagonal_first = pivot_first - corr_first
     column_second = (

time: 702 us -> 1080 us (1.54)
  waiting for transfers between devices: 637 us -> 1010 us
    psum x0 -> x2, waiting for transfers between devices: none -> 342 us  [the longest x1 260 us: body(): lax.psum(jnp.dot(own_second.T, column_second, preferred_element_type=jnp....]
    psum x1, waiting for transfers between devices: 264 us -> 281 us  [body(): lax.psum((jnp.dot(own_first.T, column_first, preferred_element_type=jnp.f...]
    reduce_scatter x2, waiting for transfers between devices: 181 us -> 195 us  [ancestor_terms(): lax.psum_scatter(summed_terms(mirrored).astype(jnp.bfloat16), 'pcol', sca...]
  transfers between devices with their start and end apart: 6 -> 8, of which waited for: 6 -> 8; matrix products, arithmetic and copies ran while one was open for 4% -> 2% of each run, Pallas kernels for 0% -> 0%
where the time goes in v1:
time: 1080 us
  waiting for transfers between devices  1010 us (94%)
  matrix products  30.5 us (3%)
  between operations  14.3 us (1%)
  other arithmetic  11.3 us (1%)
    psum x1, waiting for transfers between devices, body(): lax.psum((jnp.dot(own_first.T, column_first, preferred_element_type=jnp.f...  281 us
    psum x1, waiting for transfers between devices, body(): lax.psum(jnp.dot(own_second.T, column_second, preferred_element_type=jnp....  260 us
    reduce_scatter x2, waiting for transfers between devices, ancestor_terms(): lax.psum_scatter(summed_terms(mirrored).astype(jnp.bfloat16), 'pcol', sca...  195 us
    all_gather x2, waiting for transfers between devices, ancestor_terms(): full = lax.all_gather(local, 'pcol', axis=1, tiled=True)  116 us
    psum x1, waiting for transfers between devices, body(): lax.psum(lax.psum((jnp.dot(own_first.T, column_first, preferred_element_t...  82.2 us
    psum x1, waiting for transfers between devices, from_root(): return lax.psum(jnp.where(mine, shard, jnp.zeros_like(shard)), axis)  76 us
  transfers between devices with their start and end apart: 8, of which 8 were waited for; matrix products, arithmetic and copies ran while one was open for 2% of the time, Pallas kernels for 0%

profile of v1, /device:TPU:8, one launch (start us, length us, event | category | flops | bytes accessed | tf_op | source)
XLA Modules:
  0.0 1075.8 jit_solution(11796599344292869998)
XLA Ops:
  7.2 0.0 copy-start
  7.2 0.0 all-gather.5.cloned.1.call-start
  7.2 0.8 fusion.13
  8.0 1.5 broadcast_multiply_fusion
  9.6 0.0 all-gather.5.cloned.1.call-update
  9.6 0.0 all-gather.3.cloned.1.call-start
  9.6 1.5 broadcast_multiply_fusion.1
  11.2 0.0 all-gather.3.cloned.1.call-update
  11.2 0.0 all-reduce.14.cloned.1.call-start
  11.3 59.7 %all-gather.5.cloned.1.call-done = bf16[3072,512]{0,1:T(8,128)(2,1)} async-done(((bf16[3072,16]{0,1:T(8,128)(2,1)}), bf16[3072,512]{0,1:T(8,128)(2,1)}) %all-gather.5.cloned.1.call-update) | async-done | bytes 3145744 | tf_op jit(solution)/shard_map/all_gather | solution.py:60
  71.0 2.1 dynamic-slice_select_fusion
  73.2 55.8 %all-gather.3.cloned.1.call-done = bf16[3072,512]{0,1:T(8,128)(2,1)} async-done(((bf16[3072,16]{0,1:T(8,128)(2,1)}), bf16[3072,512]{0,1:T(8,128)(2,1)}) %all-gather.3.cloned.1.call-update) | async-done | bytes 3145744 | tf_op jit(solution)/shard_map/all_gather | solution.py:60
  129.0 2.1 dynamic-slice_select_fusion.1
  131.1 0.0 all-reduce.14.cloned.1.call-update
  131.2 0.0 reduce-scatter.3.cloned.1.call-start
  131.2 0.8 dynamic-slice_convert_fusion.2
  132.0 2.5 mul.55
  134.5 3.0 copy.18
  137.5 76.0 %all-reduce.14.cloned.1.call-done = (bf16[768,512]{0,1:T(8,128)(2,1)}, bf16[768,512]{0,1:T(8,128)(2,1)}) async-done(((bf16[768,512]{0,1:T(8,128)(2,1)}, bf16[768,512]{0,1:T(8,128)(2,1)}), (bf16[768,512]{0,1:T(8,128)(2,1)}, bf16[768,512]{0,1:T(8,128)(2,1)})) %all-reduce.14.cloned.1.call-update) | async-done | bytes 1572880 | tf_op jit(solution)/shard_map/psum | solution.py:11
  213.4 8.3 convolution_convert_fusion.1
  221.7 0.0 reduce-scatter.3.cloned.1.call-update
  221.8 0.0 all-reduce.10.cloned.1.call-start
  221.8 96.9 %reduce-scatter.3.cloned.1.call-done = bf16[96,512]{1,0:T(8,128)(2,1)} async-done(((bf16[3072,512]{1,0:T(8,128)(2,1)}), bf16[96,512]{1,0:T(8,128)(2,1)}) %reduce-scatter.3.cloned.1.call-update) | async-done | bytes 98320 | tf_op jit(solution)/shard_map/reduce_scatter | solution.py:64
  318.8 0.9 negate_convert_fusion
  319.7 0.0 copy-start.3
  319.7 2.3 fusion.11
  322.0 2.3 fusion.7
  324.3 0.0 all-reduce.10.cloned.1.call-update
  324.3 0.0 reduce-scatter.5.cloned.1.call-start
  324.4 8.0 convolution_convert_fusion
  332.3 0.0 reduce-scatter.5.cloned.1.call-update
  332.4 0.0 all-reduce.12.cloned.1.call-start
  332.4 281.5 %all-reduce.10.cloned.1.call-done = (f32[512,512]{1,0:T(8,128)}, f32[512,512]{1,0:T(8,128)}) async-done(((f32[512,512]{1,0:T(8,128)}, f32[512,512]{1,0:T(8,128)}), (f32[512,512]{1,0:T(8,128)}, f32[512,512]{1,0:T(8,128)})) %all-reduce.10.cloned.1.call-update) | async-done | bytes 2097168 | tf_op jit(solution)/shard_map/psum | solution.py:75
  613.9 0.0 all-reduce.12.cloned.1.call-update
  613.9 0.2 all-reduce.8.cloned.1.call-start
  614.1 97.9 %reduce-scatter.5.cloned.1.call-done = bf16[96,512]{1,0:T(8,128)(2,1)} async-done(((bf16[3072,512]{1,0:T(8,128)(2,1)}), bf16[96,512]{1,0:T(8,128)(2,1)}) %reduce-scatter.5.cloned.1.call-update) | async-done | bytes 98320 | tf_op jit(solution)/shard_map/reduce_scatter | solution.py:64
  712.1 1.1 fusion.6
  713.2 0.0 copy-start.6
  713.2 2.4 fusion.9
  715.6 0.0 all-reduce.8.cloned.1.call-update
  715.6 1.3 copy.14
  716.9 82.2 %all-reduce.12.cloned.1.call-done = (f32[512,512]{1,0:T(8,128)}, f32[512,512]{1,0:T(8,128)}) async-done(((f32[512,512]{1,0:T(8,128)}, f32[512,512]{1,0:T(8,128)}), (f32[512,512]{1,0:T(8,128)}, f32[512,512]{1,0:T(8,128)})) %all-reduce.12.cloned.1.call-update) | async-done | bytes 2097168 | tf_op jit(solution)/shard_map/psum | solution.py:74
  799.2 1.4 sub.18
  800.6 0.0 copy-start.1
  800.6 2.6 fusion.2
  803.2 259.7 %all-reduce.8.cloned.1.call-done = f32[512,512]{0,1:T(8,128)} async-done(((f32[512,512]{0,1:T(8,128)}), f32[512,512]{0,1:T(8,128)}) %all-reduce.8.cloned.1.call-update) | async-done | bytes 1048592 | tf_op jit(solution)/shard_map/psum | solution.py:90
  1062.9 3.5 fusion.4
  1066.5 2.5 copy.16
  (12 shorter events, 0.0 us)
Async XLA Ops:
  7.2 704.9 %copy-start = (bf16[512,512]{1,0:T(8,128)(2,1)S(1)}, bf16[512,512]{1,0:T(8,128)(2,1)}, u32[]{:S(2)}) copy-start(bf16[512,512]{1,0:T(8,128)(2,1)} %param.15) | copy-start | bytes 1572868
  7.2 63.8 %all-gather.5.cloned.1.call-start = ((), (), s32[]{:S(2)}) async-start(), calls=%async_computation.4 | async-start | bytes 3244032 | tf_op jit(solution)/shard_map/all_gather | solution.py:60
  9.6 119.4 %all-gather.3.cloned.1.call-start = ((), (), s32[]{:S(2)}) async-start(), calls=%async_computation.2 | async-start | bytes 3244032 | tf_op jit(solution)/shard_map/all_gather | solution.py:60
  11.2 202.2 %all-reduce.14.cloned.1.call-start = ((), (), s32[]{:S(2)}) async-start(), calls=%async_computation.9 | async-start | bytes 3145728 | tf_op jit(solution)/shard_map/psum | solution.py:11
  131.2 187.6 %reduce-scatter.3.cloned.1.call-start = ((), (), s32[]{:S(2)}) async-start(), calls=%async_computation.3 | async-start | bytes 3244032 | tf_op jit(solution)/shard_map/reduce_scatter | solution.py:64
  221.7 102.6 %copy-start.7 = (bf16[768,512]{0,1:T(8,128)(2,1)S(1)}, bf16[768,512]{0,1:T(8,128)(2,1)}, u32[]{:S(2)}) copy-start(bf16[768,512]{0,1:T(8,128)(2,1)} %get-tuple-element.15) | copy-start | bytes 2359300
  221.8 392.1 %all-reduce.10.cloned.1.call-start = ((), (), s32[]{:S(2)}) async-start(), calls=%async_computation.7 | async-start | bytes 4194304 | tf_op jit(solution)/shard_map/psum | solution.py:75
  319.7 392.4 %copy-start.3 = (bf16[96,512]{1,0:T(8,128)(2,1)}, bf16[96,512]{1,0:T(8,128)(2,1)S(1)}, u32[]{:S(2)}) copy-start(bf16[96,512]{1,0:T(8,128)(2,1)S(1)} %negate_convert_fusion) | copy-start | bytes 294916
  324.3 387.8 %reduce-scatter.5.cloned.1.call-start = ((), (), s32[]{:S(2)}) async-start(), calls=%async_computation.5 | async-start | bytes 3244032 | tf_op jit(solution)/shard_map/reduce_scatter | solution.py:64
  332.3 383.3 %copy-start.5 = (f32[512,512]{1,0:T(8,128)S(1)}, f32[512,512]{1,0:T(8,128)}, u32[]{:S(2)}) copy-start(f32[512,512]{1,0:T(8,128)} %param.17) | copy-start | bytes 3145732
  332.3 466.8 %copy-start.4 = (f32[512,512]{1,0:T(8,128)S(1)}, f32[512,512]{1,0:T(8,128)}, u32[]{:S(2)}) copy-start(f32[512,512]{1,0:T(8,128)} %param.16) | copy-start | bytes 3145732
  332.4 466.8 %all-reduce.12.cloned.1.call-start = ((), (), s32[]{:S(2)}) async-start(), calls=%async_computation.8 | async-start | bytes 4194304 | tf_op jit(solution)/shard_map/psum | solution.py:74
  613.9 449.0 %all-reduce.8.cloned.1.call-start = ((), (), s32[]{:S(2)}) async-start(), calls=%async_computation.6 | async-start | bytes 2097152 | tf_op jit(solution)/shard_map/psum | solution.py:90
  713.2 90.0 %copy-start.6 = (bf16[96,512]{1,0:T(8,128)(2,1)}, bf16[96,512]{1,0:T(8,128)(2,1)S(1)}, u32[]{:S(2)}) copy-start(bf16[96,512]{1,0:T(8,128)(2,1)S(1)} %fusion.6) | copy-start | bytes 294916
  800.6 268.4 %copy-start.1 = (f32[512,512]{1,0:T(8,128)}, f32[512,512]{1,0:T(8,128)S(1)}, u32[]{:S(2)}) copy-start(f32[512,512]{1,0:T(8,128)S(1)} %sub.18) | copy-start | bytes 3145732
  803.2 265.8 %copy-start.2 = (f32[512,512]{1,0:T(8,128)}, f32[512,512]{1,0:T(8,128)S(1)}, u32[]{:S(2)}) copy-start(f32[512,512]{1,0:T(8,128)S(1)} %fusion.2) | copy-start | bytes 3145732
Sparse Core Ops, SparseCore 0:
  11.1 59.8 all-gather.4
  74.1 54.8 all-gather.2
  132.3 81.1 all-reduce.13
  221.9 96.8 reduce-scatter.2
  324.4 289.4 all-reduce.9
  617.7 94.3 reduce-scatter.4
  715.0 84.1 all-reduce.11
  806.1 256.8 all-reduce.7
